TPU v7x, 512 devices: a whole 4x4x16 slice. The times are simulated.
512 devices in a mesh: row: 8 (over x, core), col: 16 (over z), layer: 4 (over y).
Axes of the slice: x: 4, y: 4, z: 16, core: 2. Of those that a mesh axis runs over, the one named last changes fastest.
Arguments:
- occurrences: bfloat16 [8192, 10240], P(('row', 'col', 'layer')), may hold values from -6 to 6
- idf_weight: float32 [8192], P(('row', 'col', 'layer')), may hold values from 0.25 to 2
- pattern: int32 [64, 80], replicated, may hold values 0 or 1
Outputs:
- margin: bfloat16 [10240, 10240], P('row', 'col')
All inputs are finite; a program needn't handle non-finite values.
Results may differ from a plain program's by a relative error of at most 0.0058.
Values may be sent and summed in bfloat16 or wider, within the bound.
No kernel may reach another device: no remote copies, remote signals or barrier semaphores. Data moves between devices by JAX's collectives and lax.ppermute only.
A program may use at most 64 MiB of HBM per device.

v0:
```python
import math
import jax
import jax.numpy as jnp
from jax import lax
from jax.sharding import PartitionSpec as P


def finish(partial_rows, row_start, col_start, factor):
    row_ids = row_start + lax.broadcasted_iota(jnp.int32, partial_rows.shape, 0)
    col_ids = col_start + lax.broadcasted_iota(jnp.int32, partial_rows.shape, 1)
    result = jnp.where(row_ids == col_ids, jnp.float32(0.0), partial_rows * factor)
    return result.astype(jnp.bfloat16)


def body(occurrences, idf_weight, pattern):
    owned, reads = occurrences.shape
    n_rows = lax.axis_size("row")
    n_cols = lax.axis_size("col")
    n_layers = lax.axis_size("layer")
    factor = 1.0 / math.sqrt(owned * n_rows * n_cols * n_layers)
    owner = lax.axis_index(("row", "col", "layer"))
    block_row = owner * owned // 128
    flags = lax.dynamic_slice_in_dim(pattern, block_row, 1, 0)[0]
    read_mask = jnp.repeat(flags.astype(jnp.float32), 128)
    weighted = (occurrences.astype(jnp.float32) * idf_weight[:, None] * read_mask[None, :]).astype(
        jnp.bfloat16
    )
    piece_len = reads // (n_rows * n_cols)
    reordered = (
        weighted.reshape(owned, n_cols, n_rows, piece_len)
        .transpose(0, 2, 1, 3)
        .reshape(owned, reads)
    )
    row_part, col_part = (
        lax.all_to_all(weighted, ("row", "col"), split_axis=1, concat_axis=0, tiled=True),
        lax.all_to_all(reordered, ("row", "col"), split_axis=1, concat_axis=0, tiled=True),
    )
    column_reads = lax.all_gather(col_part, "row", axis=1, tiled=True)
    partial_tile = lax.dot_general(
        lax.all_gather(row_part, "col", axis=1, tiled=True),
        column_reads,
        (((0,), (0,)), ((), ())),
        preferred_element_type=jnp.float32,
    )
    row_count = partial_tile.shape[0]
    row_start = lax.axis_index("row") * row_count
    col_start = lax.axis_index("col") * partial_tile.shape[1]
    total = lax.psum(partial_tile, "layer")
    return finish(total, row_start, col_start, factor)


def solution(mesh):
    placed = (P(("row", "col", "layer"), None), P(("row", "col", "layer")), P())
    return jax.shard_map(
        body, mesh=mesh, in_specs=placed, out_specs=P("row", "col"), check_vma=False
    )
```

profile of v0, /device:TPU:1, one launch (start us, length us, event | category | flops | bytes accessed | tf_op | source)
XLA Modules:
  0.0 287.5 jit_solution(10885676402827663510)
XLA Ops:
  6.5 0.0 all-gather.5.cloned.1.call-start
  6.5 0.7 convert_bitcast_fusion
  7.2 0.1 broadcast_bitcast_fusion
  7.3 1.1 multiply_convert_fusion
  8.4 0.6 reshape.14
  9.1 0.1 copy.9
  9.2 0.3 copy.10
  9.6 52.5 %all_to_all.38 = bf16[16,128,80]{2,0,1:T(8,128)(2,1)S(1)} all-to-all(bf16[16,128,80]{2,0,1:T(8,128)(2,1)S(1)} %copy.10), channel_id=1, replica_groups=mesh['row'=8,'col'=16,'layer'=4] {'row','col'}, dimensions={1} | all-to-all | bytes 655360 | tf_op jit(solution)/shard_map/all_to_all | solution.py:36
  62.0 0.9 copy.11
  63.0 0.0 all-gather.5.cloned.1.call-update
  63.0 0.0 all-gather.3.cloned.1.call-start
  63.0 0.6 all_to_all.28
  63.7 0.3 copy.7
  64.0 39.7 %all_to_all.39 = bf16[16,128,80]{2,0,1:T(8,128)(2,1)S(1)} all-to-all(bf16[16,128,80]{2,0,1:T(8,128)(2,1)S(1)} %copy.7), channel_id=1, replica_groups=mesh['row'=8,'col'=16,'layer'=4] {'row','col'}, dimensions={1} | all-to-all | bytes 655360 | tf_op jit(solution)/shard_map/all_to_all | solution.py:35
  103.8 0.9 copy.8
  104.7 0.0 all-gather.3.cloned.1.call-update
  104.7 0.0 all-reduce.2.cloned.1.call-start
  104.8 0.0 all-gather.5.cloned.1.call-done
  104.8 67.3 %all-gather.3.cloned.1.call-done = bf16[2048,1280]{0,1:T(8,128)(2,1)} async-done(((bf16[2048,80]{0,1:T(8,128)(2,1)}), bf16[2048,1280]{0,1:T(8,128)(2,1)}) %all-gather.3.cloned.1.call-update) | async-done | bytes 5242896 | tf_op jit(solution)/shard_map/all_gather | solution.py:40
  172.1 9.3 %fusion = f32[1280,640]{1,0:T(8,128)} fusion(bf16[2048,1280]{0,1:T(8,128)(2,1)} %all-gather.3.cloned.1.call-done, bf16[2048,640]{0,1:T(8,128)(2,1)} %all-gather.5.cloned.1.call-done), kind=kOutput, calls=%fused_computation.6 | convolution fusion | flops 3355443200 | bytes 11141120 | tf_op jit(solution)/shard_map/dot_general | solution.py:39
  181.3 0.0 all-reduce.2.cloned.1.call-update
  181.4 96.0 %all-reduce.2.cloned.1.call-done = f32[1280,640]{1,0:T(8,128)} async-done(((f32[1280,640]{1,0:T(8,128)}), f32[1280,640]{1,0:T(8,128)}) %all-reduce.2.cloned.1.call-update) | async-done | bytes 3276816 | tf_op jit(solution)/shard_map/psum | solution.py:48
  277.4 3.5 %select_convert_fusion = bf16[1280,640]{1,0:T(8,128)(2,1)} fusion(f32[1280,640]{1,0:T(8,128)} %all-reduce.2.cloned.1.call-done, s32[640]{0:T(1024)S(1)} %iota_add_fusion.1, s32[1280]{0:T(1024)S(1)} %iota_add_fusion), kind=kLoop, calls=%fused_computation | loop fusion | flops 3276800 | bytes 4922880 | tf_op jit(solution)/shard_map/convert_element_type | solution.py:12
  (2 shorter events, 0.0 us)
Async XLA Ops:
  6.5 98.3 %all-gather.5.cloned.1.call-start = ((), (), s32[]{:S(2)}) async-start(), calls=%async_computation.3 | async-start | bytes 2949120 | tf_op jit(solution)/shard_map/all_gather | solution.py:38
  63.0 109.1 %all-gather.3.cloned.1.call-start = ((), (), s32[]{:S(2)}) async-start(), calls=%async_computation.2 | async-start | bytes 5570560 | tf_op jit(solution)/shard_map/all_gather | solution.py:40
  104.7 172.7 %all-reduce.2.cloned.1.call-start = ((), (), s32[]{:S(2)}) async-start(), calls=%async_computation.4 | async-start | bytes 6553600 | tf_op jit(solution)/shard_map/psum | solution.py:48
Sparse Core Ops, SparseCore 0:
  63.1 29.0 all-gather.4
  104.9 67.1 all-gather.2
  181.5 95.8 all-reduce.1
where the time goes:
time: 288 us; the launch traced here: 287 us
  waiting for transfers between devices  163 us (57%)
  blocking collectives  92.2 us (32%)
  between operations  13.2 us (5%)
  matrix products  9.28 us (3%)
  other arithmetic  5.36 us (2%)
  local copies, waits for them, and re-layouts  4.02 us (1%)
    psum x1, waiting for transfers between devices, body(): total = lax.psum(partial_tile, 'layer')  96 us
    all_gather x1, waiting for transfers between devices, body(): lax.all_gather(row_part, 'col', axis=1, tiled=True)  67.3 us
    all_to_all x1, blocking collectives, body(): lax.all_to_all(reordered, ('row', 'col'), split_axis=1, concat_axis=0, ti...  52.5 us
    all_to_all x1, blocking collectives, body(): lax.all_to_all(weighted, ('row', 'col'), split_axis=1, concat_axis=0, til...  39.7 us
    dot_general x1, matrix products, body(): lax.dot_general(lax.all_gather(row_part, 'col', axis=1, tiled=True), colu...  9.28 us
  transfers between devices with their start and end apart: 3, of which 2 were waited for; matrix products, arithmetic and copies ran while one was open for 0% of the time, Pallas kernels for 0%

commit v1 on v0

--- a/solution.py
+++ b/solution.py
@@ -37,7 +37,9 @@
     )
     column_reads = lax.all_gather(col_part, "row", axis=1, tiled=True)
     partial_tile = lax.dot_general(
-        lax.all_gather(row_part, "col", axis=1, tiled=True),
+        jnp.concatenate(
+            lax.all_to_all(jnp.stack([row_part] * lax.axis_size("col")), "col", 0, 0), axis=1
+        ),
         column_reads,
         (((0,), (0,)), ((), ())),
         preferred_element_type=jnp.float32,

time: 288 us -> 451 us (1.57)
  waiting for transfers between devices: 163 us -> 381 us
  blocking collectives: 92.2 us -> 0 us
  starting transfers between devices: 0.09 us -> 33.4 us
    all_to_all x0 -> x3, waiting for transfers between devices: none -> 253 us  [the longest x1 190 us: body(): lax.all_to_all(jnp.stack([row_part] * lax.axis_size('col')), 'col', 0, 0)]
    all_to_all x2 -> x0, blocking collectives: 92.2 us -> none  [the longest x1 52.5 us: body(): lax.all_to_all(reordered, ('row', 'col'), split_axis=1, concat_axis=0, ti...]
    all_gather x1 -> x0, waiting for transfers between devices: 67.3 us -> none  [body(): lax.all_gather(row_part, 'col', axis=1, tiled=True)]
    all_gather x1, waiting for transfers between devices: 0.02 us -> 35.4 us  [body(): column_reads = lax.all_gather(col_part, 'row', axis=1, tiled=True)]
    all_to_all x0 -> x3, starting transfers between devices: none -> 33.3 us  [the longest x1 20.4 us: body(): lax.all_to_all(weighted, ('row', 'col'), split_axis=1, concat_axis=0, til...]
  transfers between devices with their start and end apart: 3 -> 5, of which waited for: 2 -> 5; matrix products, arithmetic and copies ran while one was open for 0% -> 1% of each run, Pallas kernels for 0% -> 0%
where the time goes in v1:
time: 451 us; the launch traced here: 450 us
  waiting for transfers between devices  381 us (84%)
  starting transfers between devices  33.4 us (7%)
  between operations  13.5 us (3%)
  matrix products  9.29 us (2%)
  local copies, waits for them, and re-layouts  7.87 us (2%)
  other arithmetic  5.36 us (1%)
    all_to_all x1, waiting for transfers between devices, body(): lax.all_to_all(jnp.stack([row_part] * lax.axis_size('col')), 'col', 0, 0)  190 us
    psum x1, waiting for transfers between devices, body(): total = lax.psum(partial_tile, 'layer')  92.6 us
    all_gather x1, waiting for transfers between devices, body(): column_reads = lax.all_gather(col_part, 'row', axis=1, tiled=True)  35.4 us
    all_to_all x1, waiting for transfers between devices, body(): lax.all_to_all(reordered, ('row', 'col'), split_axis=1, concat_axis=0, ti...  32.1 us
    all_to_all x1, waiting for transfers between devices, body(): lax.all_to_all(weighted, ('row', 'col'), split_axis=1, concat_axis=0, til...  30.4 us
    all_to_all x1, starting transfers between devices, body(): lax.all_to_all(weighted, ('row', 'col'), split_axis=1, concat_axis=0, til...  20.4 us
    dot_general x1, matrix products, body(): lax.dot_general(jnp.concatenate(lax.all_to_all(jnp.stack([row_part] * lax...  9.29 us
  transfers between devices with their start and end apart: 5, of which 5 were waited for; matrix products, arithmetic and copies ran while one was open for 1% of the time, Pallas kernels for 0%

profile of v1, /device:TPU:1, one launch (start us, length us, event | category | flops | bytes accessed | tf_op | source)
XLA Modules:
  0.0 450.2 jit_solution(14905706455424459621)
XLA Ops:
  6.5 0.7 convert_bitcast_fusion
  7.2 0.1 broadcast_bitcast_fusion
  7.3 1.1 multiply_convert_fusion
  8.4 0.6 all_to_all.29
  9.1 1.1 copy.8
  10.2 20.4 %all-to-all-start = ((bf16[16,128,80]{2,0,1:T(8,128)(2,1)}), bf16[16,128,80]{2,0,1:T(8,128)(2,1)S(1)}, u32[]{:S(2)}, u32[]{:S(2)}) async-start(bf16[16,128,80]{2,0,1:T(8,128)(2,1)} %copy.8), calls=%async_computation | async-start | bytes 1048576 | tf_op jit(solution)/shard_map/all_to_all | solution.py:35
  30.6 0.6 reshape.25
  31.3 0.1 copy.10
  31.4 1.1 copy.11
  32.5 30.4 %all-to-all-done = bf16[16,128,80]{2,0,1:T(8,128)(2,1)S(1)} async-done(((bf16[16,128,80]{2,0,1:T(8,128)(2,1)}), bf16[16,128,80]{2,0,1:T(8,128)(2,1)S(1)}, u32[]{:S(2)}, u32[]{:S(2)}) %all-to-all-start) | async-done | bytes 327712 | tf_op jit(solution)/shard_map/all_to_all | solution.py:35
  62.9 7.6 %all-to-all-start.2 = ((bf16[16,128,80]{2,0,1:T(8,128)(2,1)}), bf16[16,128,80]{2,0,1:T(8,128)(2,1)S(1)}, u32[]{:S(2)}, u32[]{:S(2)}) async-start(bf16[16,128,80]{2,0,1:T(8,128)(2,1)} %copy.11), calls=%async_computation.2 | async-start | bytes 1048576 | tf_op jit(solution)/shard_map/all_to_all | solution.py:36
  70.6 0.2 copy.9
  70.8 32.1 %all-to-all-done.2 = bf16[16,128,80]{2,0,1:T(8,128)(2,1)S(1)} async-done(((bf16[16,128,80]{2,0,1:T(8,128)(2,1)}), bf16[16,128,80]{2,0,1:T(8,128)(2,1)S(1)}, u32[]{:S(2)}, u32[]{:S(2)}) %all-to-all-start.2) | async-done | bytes 327712 | tf_op jit(solution)/shard_map/all_to_all | solution.py:36
  102.8 3.0 stack.5
  105.8 5.3 %all-to-all-start.1 = ((bf16[16,2048,80]{1,2,0:T(8,128)(2,1)}), bf16[16,2048,80]{1,2,0:T(8,128)(2,1)}, u32[]{:S(2)}, u32[]{:S(2)}) async-start(bf16[16,2048,80]{1,2,0:T(8,128)(2,1)} %stack.5), calls=%async_computation.1 | async-start | bytes 10485760 | tf_op jit(solution)/shard_map/all_to_all | solution.py:41
  111.2 0.0 all-gather.2.cloned.1.call-start
  111.2 0.9 copy.12
  112.1 0.0 all-gather.2.cloned.1.call-update
  112.2 0.0 all-reduce.2.cloned.1.call-start
  112.2 35.4 %all-gather.2.cloned.1.call-done = bf16[2048,640]{0,1:T(8,128)(2,1)} async-done(((bf16[2048,80]{0,1:T(8,128)(2,1)}), bf16[2048,640]{0,1:T(8,128)(2,1)}) %all-gather.2.cloned.1.call-update) | async-done | bytes 2621456 | tf_op jit(solution)/shard_map/all_gather | solution.py:38
  147.6 190.2 %all-to-all-done.1 = bf16[16,2048,80]{1,2,0:T(8,128)(2,1)} async-done(((bf16[16,2048,80]{1,2,0:T(8,128)(2,1)}), bf16[16,2048,80]{1,2,0:T(8,128)(2,1)}, u32[]{:S(2)}, u32[]{:S(2)}) %all-to-all-start.1) | async-done | bytes 5242912 | tf_op jit(solution)/shard_map/all_to_all | solution.py:41
  337.9 9.3 %fusion = f32[1280,640]{1,0:T(8,128)} fusion(bf16[2048,1280]{0,1:T(8,128)(2,1)} %bitcast.5, bf16[2048,640]{0,1:T(8,128)(2,1)} %all-gather.2.cloned.1.call-done), kind=kOutput, calls=%fused_computation.6 | convolution fusion | flops 3355443200 | bytes 11141120 | tf_op jit(solution)/shard_map/dot_general | solution.py:39
  347.1 0.0 all-reduce.2.cloned.1.call-update
  347.2 92.6 %all-reduce.2.cloned.1.call-done = f32[1280,640]{1,0:T(8,128)} async-done(((f32[1280,640]{1,0:T(8,128)}), f32[1280,640]{1,0:T(8,128)}) %all-reduce.2.cloned.1.call-update) | async-done | bytes 3276816 | tf_op jit(solution)/shard_map/psum | solution.py:50
  439.8 3.5 select_convert_fusion
  (2 shorter events, 0.0 us)
Async XLA Ops:
  10.2 52.7 %all-to-all-start = ((bf16[16,128,80]{2,0,1:T(8,128)(2,1)}), bf16[16,128,80]{2,0,1:T(8,128)(2,1)S(1)}, u32[]{:S(2)}, u32[]{:S(2)}) async-start(bf16[16,128,80]{2,0,1:T(8,128)(2,1)} %copy.8), calls=%async_computation | async-start | bytes 1048576 | tf_op jit(solution)/shard_map/all_to_all | solution.py:35
  62.9 39.9 %all-to-all-start.2 = ((bf16[16,128,80]{2,0,1:T(8,128)(2,1)}), bf16[16,128,80]{2,0,1:T(8,128)(2,1)S(1)}, u32[]{:S(2)}, u32[]{:S(2)}) async-start(bf16[16,128,80]{2,0,1:T(8,128)(2,1)} %copy.11), calls=%async_computation.2 | async-start | bytes 1048576 | tf_op jit(solution)/shard_map/all_to_all | solution.py:36
  105.8 232.0 %all-to-all-start.1 = ((bf16[16,2048,80]{1,2,0:T(8,128)(2,1)}), bf16[16,2048,80]{1,2,0:T(8,128)(2,1)}, u32[]{:S(2)}, u32[]{:S(2)}) async-start(bf16[16,2048,80]{1,2,0:T(8,128)(2,1)} %stack.5), calls=%async_computation.1 | async-start | bytes 10485760 | tf_op jit(solution)/shard_map/all_to_all | solution.py:41
  111.2 36.5 %all-gather.2.cloned.1.call-start = ((), (), s32[]{:S(2)}) async-start(), calls=%async_computation.3 | async-start | bytes 2949120 | tf_op jit(solution)/shard_map/all_gather | solution.py:38
  112.2 327.6 %all-reduce.2.cloned.1.call-start = ((), (), s32[]{:S(2)}) async-start(), calls=%async_computation.4 | async-start | bytes 6553600 | tf_op jit(solution)/shard_map/psum | solution.py:50
Sparse Core Ops, SparseCore 0:
  114.1 33.4 all-gather.1
  347.3 92.4 all-reduce.1
